TPU v7x, 512 devices: a whole 4x4x16 slice. The times are simulated.
512 devices in a mesh: row: 32 (over x, y, core), layer: 16 (over z).
Axes of the slice: x: 4, y: 4, z: 16, core: 2. Of those that a mesh axis runs over, the one named last changes fastest.
Arguments:
- rhs_local: bfloat16 [16, 2, 1024, 256], P('layer', None, 'row'), may hold values from -6 to 6
- dinv_local: bfloat16 [16, 2, 1024, 1024], P('layer', None, 'row')
- lower_anc: bfloat16 [16, 2, 1024, 1024], P('layer', None, 'row'), may hold values from -0.03125 to 0.03125
- lower_high: bfloat16 [16, 2, 32768, 1024], P('layer', None, 'row'), may hold values from -0.046875 to 0.046875
- row_blocks: int32 [16, 2, 256], P('layer', None, 'row'), may hold values from 0 to 15
- rhs_anc: float32 [1024, 256], P('row'), may hold values from -6 to 6
- rhs_high: float32 [65536, 256], P(('row', 'layer')), may hold values from -6 to 6
- dinv_anc: bfloat16 [1024, 1024], P('row')
- lower_anc_high: bfloat16 [65536, 1024], P(('row', 'layer')), may hold values from -0.1875 to 0.1875
Outputs:
- sol_local: bfloat16 [16, 2, 1024, 256], P('layer', None, 'row')
- sol_anc: bfloat16 [1024, 256], P('row')
- high_out: float32 [65536, 256], P(('row', 'layer'))
Inputs may be any that keep to these rules, and one draw needn't show every extreme that they name: Row index block q of lower_high, held by row index g = q // 8, lands in block row_blocks of that index's 16 blocks of higher ancestor rows.
All inputs are finite; a program needn't handle non-finite values.
Results may differ from a plain program's by a relative error of at most 0.008.
Values may be sent and summed in bfloat16 or wider, within the bound.
A program may use at most 64 MiB of HBM per device.

v0:
```python
import jax
import jax.numpy as jnp
from jax import lax
from jax.sharding import PartitionSpec as P

BLOCK = 128
HBLK = 16


def copy_for_each(shard, axis):
    count = lax.axis_size(axis)
    return lax.all_to_all(
        jnp.broadcast_to(shard[None], (count, *shard.shape)), axis, 0, 0, tiled=True
    )


def joined_along(parts, dim):
    parts = jnp.moveaxis(parts, 0, dim)
    dims = parts.shape
    return parts.reshape(*dims[:dim], dims[dim] * dims[dim + 1], *dims[dim + 2 :])


def gather_directly(shard, axis, dim):
    parts = copy_for_each(shard, axis)
    return joined_along(parts, dim)


def of_everyone(shard, axis):
    return copy_for_each(shard, axis).sum(axis=0)


def on_device(
    rhs_local,
    dinv_local,
    lower_anc,
    lower_high,
    row_blocks,
    rhs_anc,
    rhs_high,
    dinv_anc,
    lower_anc_high,
):
    rhs_mine = rhs_local[0]
    dinv_mine = dinv_local[0]
    anc_mine = lower_anc[0]
    high_mine = lower_high[0]
    blocks_mine = row_blocks[0]
    width = rhs_mine.shape[2]
    columns = dinv_mine
    local_acc = jnp.einsum(
        "sik,skc->sic",
        columns,
        gather_directly(rhs_mine, "row", 1),
        preferred_element_type=jnp.float32,
    )
    sol_mine = local_acc.astype(jnp.bfloat16)
    portion = gather_directly(sol_mine, "row", 1)
    anc_next = jnp.einsum("sik,skc->ic", anc_mine, portion, preferred_element_type=jnp.float32)
    high_next = jnp.einsum("sik,skc->sic", high_mine, portion, preferred_element_type=jnp.float32)
    supers = high_mine.shape[0]
    blocks_held = blocks_mine.shape[1]
    one_hot = (blocks_mine[:, :, None] == jnp.arange(HBLK, dtype=jnp.int32)[None, None, :]).astype(
        jnp.float32
    )
    high_blocks = high_next.reshape(supers, blocks_held, BLOCK, width)
    high_part = jnp.einsum(
        "sqh,sqpc->hpc", one_hot, high_blocks, precision=lax.Precision.HIGHEST
    ).reshape(HBLK * BLOCK, width)
    anc_sum = of_everyone(anc_next, "layer")
    high_sum = lax.psum_scatter(
        high_part.astype(jnp.bfloat16), "layer", scatter_dimension=0, tiled=True
    ).astype(jnp.float32)
    anc_rhs = (rhs_anc - anc_sum).astype(jnp.bfloat16)
    columns = dinv_anc
    anc_acc = jnp.dot(
        columns,
        lax.all_gather(anc_rhs, "row", axis=0, tiled=True),
        preferred_element_type=jnp.float32,
    )
    anc_solved = anc_acc.astype(jnp.bfloat16)
    columns = lower_anc_high
    reach_terms = jnp.dot(
        columns,
        lax.all_gather(anc_solved, "row", axis=0, tiled=True),
        preferred_element_type=jnp.float32,
    )
    high_new = rhs_high - high_sum - reach_terms
    return (sol_mine[None], anc_solved, high_new)


def solution(mesh):
    return jax.shard_map(
        on_device,
        mesh=mesh,
        in_specs=(
            P("layer", None, "row", None),
            P("layer", None, "row", None),
            P("layer", None, "row", None),
            P("layer", None, "row", None),
            P("layer", None, "row"),
            P("row", None),
            P(("row", "layer"), None),
            P("row", None),
            P(("row", "layer"), None),
        ),
        out_specs=(P("layer", None, "row", None), P("row", None), P(("row", "layer"), None)),
        check_vma=False,
    )
```

profile of v0, /device:TPU:1, one launch (start us, length us, event | category | flops | bytes accessed | tf_op | source)
XLA Modules:
  0.0 156.5 jit_solution(8813639736755442857)
XLA Ops:
  7.2 0.0 copy-start
  7.2 0.9 broadcast_in_dim.11
  8.1 0.0 copy-start.1
  8.1 26.6 %all_to_all.15 = bf16[32,2,32,256]{3,2,1,0:T(8,128)(2,1)S(1)} all-to-all(bf16[32,2,32,256]{3,2,1,0:T(8,128)(2,1)S(1)} %broadcast_in_dim.11), channel_id=1, replica_groups=mesh['row'=32,'layer'=16] {'row'}, dimensions={0} | all-to-all | bytes 2097152 | tf_op jit(solution)/shard_map/all_to_all | solution.py:12
  34.8 0.1 copy.32
  34.8 0.0 copy-done.1
  34.8 0.3 convolution_convert_fusion
  35.1 0.0 copy-start.3
  35.1 0.1 broadcast_in_dim.26
  35.3 0.0 copy-start.2
  35.3 20.7 %all_to_all.16 = bf16[32,2,32,256]{3,2,1,0:T(8,128)(2,1)S(1)} all-to-all(bf16[32,2,32,256]{3,2,1,0:T(8,128)(2,1)S(1)} %broadcast_in_dim.26), channel_id=1, replica_groups=mesh['row'=32,'layer'=16] {'row'}, dimensions={0} | all-to-all | bytes 2097152 | tf_op jit(solution)/shard_map/all_to_all | solution.py:12
  56.0 0.1 copy.33
  56.1 0.0 copy-done.3
  56.1 0.0 copy-done.2
  56.1 0.3 convolution_bitcast_fusion.1
  56.4 0.9 broadcast_in_dim.27
  57.3 13.7 %all-to-all-start.2 = ((f32[16,32,256]{2,1,0:T(8,128)}), f32[16,32,256]{2,1,0:T(8,128)S(1)}, u32[]{:S(2)}, u32[]{:S(2)}) async-start(f32[16,32,256]{2,1,0:T(8,128)} %broadcast_in_dim.27), calls=%async_computation.2 | async-start | bytes 1048576 | tf_op jit(solution)/shard_map/all_to_all | solution.py:12
  71.0 0.0 reduce-scatter.4.cloned.1.call-start
  71.1 3.6 %fusion = f32[2,256,1024]{2,1,0:T(8,128)S(1)} fusion(bf16[2,1024,256]{2,1,0:T(8,128)(2,1)S(1)} %bitcast.51, bf16[1,2,1024,1024]{3,2,1,0:T(8,128)(2,1)} %param.12), kind=kOutput, calls=%fused_computation | convolution fusion | flops 1073741824 | bytes 7340032 | tf_op jit(solution)/shard_map/sik,skc->sic/dot_general | solution.py:59
  74.7 0.5 copy.44
  75.1 0.0 copy-start.8
  75.1 2.1 %copy.35 = f32[2,8,128,256]{3,1,0,2:T(8,128)} copy(f32[2,8,128,256]{2,1,3,0:T(8,128)S(1)} %bitcast.53) | data formatting | bytes 4194304 | tf_op jit(solution)/shard_map/reshape | solution.py:65
  77.3 0.0 copy-done.8
  77.3 2.8 %bitcast_convert_fusion = bf16[16,128,256]{2,0,1:T(8,128)(2,1)S(1)} fusion(f32[2,8,128,256]{3,1,0,2:T(8,128)} %copy.35, s32[2,8]{1,0:T(2,128)S(1)} %bitcast.59), kind=kOutput, calls=%fused_computation.2 | convolution fusion | flops 101187840 | bytes 3145792 | tf_op jit(solution)/shard_map/sqh,sqpc->hpc/dot_general | solution.py:66
  80.1 0.0 copy-start.4
  80.1 0.0 copy-start.7
  80.1 0.0 copy-start.5
  80.1 1.3 copy.36
  81.4 0.0 reduce-scatter.4.cloned.1.call-update
  81.5 0.0 copy-done.4
  81.5 0.1 copy.38
  81.6 12.5 %all-to-all-done.2 = f32[16,32,256]{2,1,0:T(8,128)S(1)} async-done(((f32[16,32,256]{2,1,0:T(8,128)}), f32[16,32,256]{2,1,0:T(8,128)S(1)}, u32[]{:S(2)}, u32[]{:S(2)}) %all-to-all-start.2) | async-done | bytes 524320 | tf_op jit(solution)/shard_map/all_to_all | solution.py:12
  94.1 0.0 copy-done.7
  94.1 29.8 %all_gather.6 = bf16[1024,256]{1,0:T(8,128)(2,1)S(1)} all-gather(bf16[32,256]{1,0:T(8,128)(2,1)S(1)} %subtract_convert_fusion), channel_id=1, replica_groups=mesh['row'=32,'layer'=16] {'row'}, dimensions={0}, use_global_device_ids=true | all-gather | bytes 540672 | tf_op jit(solution)/shard_map/all_gather | solution.py:77
  123.9 0.0 copy-done.5
  123.9 0.2 fusion.3
  124.1 0.0 copy-start.6
  124.1 23.5 %all_gather.7 = bf16[1024,256]{1,0:T(8,128)(2,1)S(1)} all-gather(bf16[32,256]{1,0:T(8,128)(2,1)S(1)} %fusion.3), channel_id=1, replica_groups=mesh['row'=32,'layer'=16] {'row'}, dimensions={0}, use_global_device_ids=true | all-gather | bytes 540672 | tf_op jit(solution)/shard_map/all_gather | solution.py:84
  147.6 0.0 reduce-scatter.4.cloned.1.call-done
  147.6 0.9 copy.43
  148.5 0.0 copy-done
  148.5 0.3 fusion.2
  148.9 0.8 copy.39
  149.6 0.0 copy-done.6
  (2 shorter events, 0.0 us)
Async XLA Ops:
  7.2 141.4 %copy-start = (bf16[128,1024]{1,0:T(8,128)(2,1)S(1)}, bf16[128,1024]{1,0:T(8,128)(2,1)}, u32[]{:S(2)}) copy-start(bf16[128,1024]{1,0:T(8,128)(2,1)} %param.17) | copy-start | bytes 786436
  8.1 26.7 %copy-start.1 = (bf16[1,2,32,1024]{3,2,1,0:T(8,128)(2,1)S(1)}, bf16[1,2,32,1024]{3,2,1,0:T(8,128)(2,1)}, u32[]{:S(2)}) copy-start(bf16[1,2,32,1024]{3,2,1,0:T(8,128)(2,1)} %param.10) | copy-start | bytes 393220
  35.1 21.0 %copy-start.3 = (bf16[2,32,256]{2,1,0:T(8,128)(2,1)}, bf16[2,32,256]{2,1,0:T(8,128)(2,1)S(1)}, u32[]{:S(2)}) copy-start(bf16[2,32,256]{2,1,0:T(8,128)(2,1)S(1)} %convolution_convert_fusion) | copy-start | bytes 98308
  35.3 20.9 %copy-start.2 = (bf16[1,2,32,1024]{3,2,1,0:T(8,128)(2,1)S(1)}, bf16[1,2,32,1024]{3,2,1,0:T(8,128)(2,1)}, u32[]{:S(2)}) copy-start(bf16[1,2,32,1024]{3,2,1,0:T(8,128)(2,1)} %param.11) | copy-start | bytes 393220
  57.3 36.8 %all-to-all-start.2 = ((f32[16,32,256]{2,1,0:T(8,128)}), f32[16,32,256]{2,1,0:T(8,128)S(1)}, u32[]{:S(2)}, u32[]{:S(2)}) async-start(f32[16,32,256]{2,1,0:T(8,128)} %broadcast_in_dim.27), calls=%async_computation.2 | async-start | bytes 1048576 | tf_op jit(solution)/shard_map/all_to_all | solution.py:12
  71.0 76.6 %reduce-scatter.4.cloned.1.call-start = ((), (), s32[]{:S(2)}) async-start(), calls=%async_computation.4 | async-start | bytes 1114112
  75.1 2.2 %copy-start.8 = (s32[1,2,8]{2,1,0:T(2,128)S(1)}, s32[1,2,8]{2,1,0:T(2,128)}, u32[]{:S(2)}) copy-start(s32[1,2,8]{2,1,0:T(2,128)} %param.13) | copy-start | bytes 196
  80.1 1.4 copy-start.4
  80.1 14.0 %copy-start.7 = (f32[32,256]{1,0:T(8,128)S(1)}, f32[32,256]{1,0:T(8,128)}, u32[]{:S(2)}) copy-start(f32[32,256]{1,0:T(8,128)} %param.14) | copy-start | bytes 98308
  80.1 43.8 %copy-start.5 = (bf16[32,1024]{1,0:T(8,128)(2,1)S(1)}, bf16[32,1024]{1,0:T(8,128)(2,1)}, u32[]{:S(2)}) copy-start(bf16[32,1024]{1,0:T(8,128)(2,1)} %param.16) | copy-start | bytes 196612
  124.1 25.6 %copy-start.6 = (bf16[32,256]{1,0:T(8,128)(2,1)}, bf16[32,256]{1,0:T(8,128)(2,1)S(1)}, u32[]{:S(2)}) copy-start(bf16[32,256]{1,0:T(8,128)(2,1)S(1)} %fusion.3) | copy-start | bytes 49156
Sparse Core Ops, SparseCore 0:
  81.6 58.8 reduce-scatter.3
where the time goes:
time: 159 us; the launch traced here: 156 us
  blocking collectives  101 us (64%)
  between operations  14.2 us (9%)
  starting transfers between devices  13.8 us (9%)
  waiting for transfers between devices  12.5 us (8%)
  local copies, waits for them, and re-layouts  7.86 us (5%)
  matrix products  7.46 us (5%)
    all_to_all x2, blocking collectives, copy_for_each(): lax.all_to_all(jnp.broadcast_to(shard[None], (count, *shard.shape)), axis...  47.4 us
    all_gather x1, blocking collectives, on_device(): lax.all_gather(anc_rhs, 'row', axis=0, tiled=True)  29.8 us
    all_gather x1, blocking collectives, on_device(): lax.all_gather(anc_solved, 'row', axis=0, tiled=True)  23.5 us
    all_to_all x1, starting transfers between devices, copy_for_each(): lax.all_to_all(jnp.broadcast_to(shard[None], (count, *shard.shape)), axis...  13.7 us
    all_to_all x1, waiting for transfers between devices, copy_for_each(): lax.all_to_all(jnp.broadcast_to(shard[None], (count, *shard.shape)), axis...  12.5 us
    dot_general x1, matrix products, on_device(): jnp.einsum('sik,skc->sic', high_mine, portion, preferred_element_type=jnp...  3.59 us
  transfers between devices with their start and end apart: 2, of which 1 were waited for; matrix products, arithmetic and copies ran while one was open for 7% of the time, Pallas kernels for 0%

commit v1 on v0

v1 whole, which is shorter than its diff:
```python
import functools

import jax
import jax.numpy as jnp
from jax import lax
from jax.experimental import pallas as pl
from jax.experimental.pallas import tpu as pltpu
from jax.sharding import PartitionSpec as P

BLOCK = 128
HBLK = 16
X, Y, CORES = 4, 4, 2
NEAR_FIRST = (1, 3, 2)
PIECES = 4
STOP = 99


class Copies:
    def __init__(self, send_sem, recv_sem):
        self.send_sem, self.recv_sem = send_sem, recv_sem
        self.used = 0
        self.started = []

    def take(self, count=1):
        first = self.used
        self.used += count
        return first

    def start(self, index, src, dst, device):
        copy = pltpu.make_async_remote_copy(
            src_ref=src,
            dst_ref=dst,
            send_sem=self.send_sem.at[index],
            recv_sem=self.recv_sem.at[index],
            device_id=device,
            device_id_type=pl.DeviceIdType.MESH,
        )
        copy.start()
        self.started.append(copy)

    def arrived(self, index, dst, device):
        pltpu.make_async_remote_copy(
            src_ref=dst,
            dst_ref=dst,
            send_sem=self.send_sem.at[index],
            recv_sem=self.recv_sem.at[index],
            device_id=device,
            device_id_type=pl.DeviceIdType.MESH,
        ).wait_recv()

    def drain(self):
        for copy in self.started:
            copy.wait_send()
        self.started = []


class Place:
    def __init__(self):
        row = lax.axis_index("row")
        self.row = row
        self.x = row // (Y * CORES)
        self.y = (row // CORES) % Y
        self.core = row % CORES

    def at(self, dx, dy, flip=False):
        x = lax.rem(self.x + (dx + X), X)
        y = lax.rem(self.y + (dy + Y), Y)
        core = 1 - self.core if flip else self.core
        return (x * Y + y) * CORES + core


class TreeGather:
    def __init__(self, copies, place, half, both):
        self.copies, self.place, self.half, self.both = copies, place, half, both
        self.first = {(h, d): copies.take() for h in (0, 1) for d in (1, 2, 3)}
        self.second = {
            (h, e, d): copies.take() for h in (0, 1) for e in range(4) for d in (1, 2, 3)
        }
        self.other = {(dx, dy): copies.take() for dx in range(X) for dy in range(Y)}

    def along(self, h, d, e):
        return (d, e) if h == 0 else (e, d)

    def send_first(self, h, d):
        at = self.place.at
        shard = self.half(h, at(0, 0))
        self.copies.start(self.first[h, d], shard, shard, {"row": at(*self.along(h, d, 0))})

    def send_second(self, h, e):
        at = self.place.at
        shard = self.half(h, at(*self.along(h, -e, 0)))
        for d in NEAR_FIRST:
            self.copies.start(
                self.second[h, e, d], shard, shard, {"row": at(*self.along(h, 0, d))}
            )

    def send_other(self, dx, dy):
        at = self.place.at
        shard = self.both(at(-dx, -dy))
        self.copies.start(self.other[dx, dy], shard, shard, {"row": at(0, 0, True)})

    def start(self):
        for d in NEAR_FIRST:
            for h in (0, 1):
                self.send_first(h, d)
        for h in (0, 1):
            self.send_second(h, 0)
        self.send_other(0, 0)

    def finish(self):
        at = self.place.at
        for e in NEAR_FIRST:
            for h in (0, 1):
                self.copies.arrived(
                    self.first[h, e],
                    self.half(h, at(*self.along(h, -e, 0))),
                    {"row": at(*self.along(h, -e, 0))},
                )
                self.send_second(h, e)
        order = [(dx, dy) for dx in range(X) for dy in range(Y) if dx or dy]
        order.sort(key=lambda p: (min(p[0], X - p[0]) + min(p[1], Y - p[1]), p))
        for dx, dy in order:
            source = at(-dx, -dy)
            if dy:
                self.copies.arrived(
                    self.second[0, dx, dy], self.half(0, source), {"row": at(0, -dy)}
                )
            if dx:
                self.copies.arrived(
                    self.second[1, dy, dx], self.half(1, source), {"row": at(-dx, 0)}
                )
            self.send_other(dx, dy)
        for dx, dy in [(0, 0)] + order:
            self.copies.arrived(
                self.other[dx, dy], self.both(at(-dx, -dy, True)), {"row": at(0, 0, True)}
            )


class DirectGather:
    def __init__(self, copies, place, shard):
        self.copies, self.place, self.shard = copies, place, shard
        self.order = [(dx, dy) for dx in range(X) for dy in range(Y) if dx or dy]
        self.order.sort(key=lambda p: (min(p[0], X - p[0]) + min(p[1], Y - p[1]), p))
        self.peer = {p: copies.take() for p in self.order}
        self.other = {p: copies.take() for p in [(0, 0)] + self.order}

    def start(self):
        at = self.place.at
        mine = self.shard(at(0, 0))
        for p in reversed(self.order):
            self.copies.start(self.peer[p], mine, mine, {"row": at(*p)})
        self.send_other(0, 0)

    def send_other(self, dx, dy):
        at = self.place.at
        shard = self.shard(at(-dx, -dy))
        self.copies.start(self.other[dx, dy], shard, shard, {"row": at(0, 0, True)})

    def finish(self):
        at = self.place.at
        for dx, dy in self.order:
            self.copies.arrived(
                self.peer[dx, dy], self.shard(at(-dx, -dy)), {"row": at(-dx, -dy)}
            )
            self.send_other(dx, dy)
        for dx, dy in [(0, 0)] + self.order:
            self.copies.arrived(
                self.other[dx, dy], self.shard(at(-dx, -dy, True)), {"row": at(0, 0, True)}
            )


def dot(a, b):
    return jnp.dot(a, b, preferred_element_type=jnp.float32)


def kernel(
    layers,
    blocks_ref,
    rhs_hbm,
    dinv_hbm,
    anc_hbm,
    high_hbm,
    rhs_anc_hbm,
    rhs_high_hbm,
    dinv_anc_hbm,
    lower_hbm,
    sol_out,
    anc_out,
    high_out,
    dinv,
    anc,
    high,
    rhs_anc,
    rhs_high,
    dinv_anc,
    lower,
    rhs_all,
    sol_all,
    anc_all,
    anc_sol_all,
    partial,
    product,
    up_in,
    up_out,
    down_in,
    down_out,
    anc_near,
    anc_far,
    anc_own,
    result,
    before,
    send_sem,
    recv_sem,
    local_sem,
):
    place = Place()
    row = place.row
    layer = lax.axis_index("layer")
    copies = Copies(send_sem, recv_sem)
    supers, rows, width = sol_out.shape[1:]
    held = supers * blocks_ref.shape[2]
    anc_rows = rhs_anc.shape[0]

    def layer_at(step):
        return lax.rem(layer + (step + layers), layers)

    def span(r, count):
        return pl.ds(pl.multiple_of(r * count, count), count)

    def half_of(ref):
        return lambda h, r: ref.at[h, span(r, rows), :]

    def both_of(ref):
        return lambda r: ref.at[:, span(r, rows), :]

    loads = []
    for n, (src, dst) in enumerate(
        (
            (rhs_hbm.at[0], rhs_all.at[:, span(row, rows), :]),
            (dinv_hbm.at[0], dinv),
            (anc_hbm.at[0], anc),
            (high_hbm.at[0], high),
            (rhs_anc_hbm, rhs_anc),
            (rhs_high_hbm, rhs_high),
            (dinv_anc_hbm, dinv_anc),
            (lower_hbm, lower),
        )
    ):
        load = pltpu.make_async_copy(src, dst, local_sem.at[n])
        load.start()
        loads.append(load)

    barrier = pltpu.get_barrier_semaphore()
    plane = [(dx, dy) for dx in range(X) for dy in range(Y) if dx or dy]
    along = [1, -1, 2, -2, 4, -4, 8]
    for dx, dy in plane:
        pl.semaphore_signal(
            barrier, inc=1, device_id={"row": place.at(dx, dy)}, device_id_type=pl.DeviceIdType.MESH
        )
    pl.semaphore_signal(
        barrier, inc=1, device_id={"row": place.at(0, 0, True)}, device_id_type=pl.DeviceIdType.MESH
    )
    for step in along:
        pl.semaphore_signal(
            barrier, inc=1, device_id={"layer": layer_at(step)}, device_id_type=pl.DeviceIdType.MESH
        )

    home = [blocks_ref[0, i // (held // supers), i % (held // supers)] for i in range(held)]
    for i in range(held):
        last = jnp.int32(held)
        for j in range(i):
            last = jnp.where(home[j] == home[i], j, last)
        before[i] = last
    partial[held] = jnp.zeros_like(partial[held])

    loads[0].wait()
    pl.semaphore_wait(barrier, len(plane) + 1 + len(along))

    gather_rhs = TreeGather(copies, place, half_of(rhs_all), both_of(rhs_all))
    gather_rhs.start()
    gather_rhs.finish()
    loads[1].wait()
    for s in range(supers):
        sol_all[s, span(row, rows), :] = dot(dinv[s], rhs_all[s]).astype(jnp.bfloat16)
    gather_sol = TreeGather(copies, place, half_of(sol_all), both_of(sol_all))
    gather_sol.start()
    store_sol = pltpu.make_async_copy(
        sol_all.at[:, span(row, rows), :], sol_out.at[0], local_sem.at[8]
    )
    store_sol.start()
    gather_sol.finish()

    loads[2].wait()
    own = dot(anc[0], sol_all[0])
    for s in range(1, supers):
        own += dot(anc[s], sol_all[s])
    anc_own[0] = own.astype(jnp.bfloat16)
    near = {step: copies.take() for step in (1, -1, -2)}
    for n, step in enumerate(near):
        copies.start(near[step], anc_own.at[0], anc_near.at[n], {"layer": layer_at(step)})

    loads[3].wait()
    for s in range(supers):
        product[...] = dot(high[s], sol_all[s])
        for q in range(held // supers):
            i = s * (held // supers) + q
            partial[i] = product[q * BLOCK : (q + 1) * BLOCK, :] + partial[before[i]]

    def slot_of(h):
        last = jnp.int32(held)
        for i in range(held):
            last = jnp.where(home[i] == h, i, last)
        return last

    cut = BLOCK // PIECES
    ups, downs = layers // 2, layers // 2 - 1
    up = {(t, p): copies.take() for t in range(ups) for p in range(PIECES)}
    down = {(t, p): copies.take() for t in range(downs) for p in range(PIECES)}

    def reduce_step(t):
        lanes = []
        if t < ups:
            lanes.append((up, up_in, up_out, 1, layer_at(ups - t)))
        if t < downs:
            lanes.append((down, down_in, down_out, -1, layer_at(t - downs)))
        slots = [slot_of(h) for *_, h in lanes]
        for p in range(PIECES):
            piece = pl.ds(p * cut, cut)
            for (index, inbox, outbox, step, _), slot in zip(lanes, slots):
                value = partial[slot, piece, :]
                if t:
                    copies.arrived(
                        index[t - 1, p], inbox.at[t - 1, piece, :], {"layer": layer_at(-step)}
                    )
                    value = value + inbox[t - 1, piece, :].astype(jnp.float32)
                outbox[t, piece, :] = value.astype(jnp.bfloat16)
                copies.start(
                    index[t, p],
                    outbox.at[t, piece, :],
                    inbox.at[t, piece, :],
                    {"layer": layer_at(step)},
                )

    reduce_step(0)

    for n, step in enumerate(near):
        copies.arrived(near[step], anc_near.at[n], {"layer": layer_at(-step)})
        own = own + anc_near[n].astype(jnp.float32)
    anc_own[1] = own.astype(jnp.bfloat16)
    far = {step: copies.take() for step in (8, 4, -4)}
    for n, step in enumerate(far):
        copies.start(far[step], anc_own.at[1], anc_far.at[n], {"layer": layer_at(step)})

    for t in (1, 2, 3):
        reduce_step(t)

    for n, step in enumerate(far):
        copies.arrived(far[step], anc_far.at[n], {"layer": layer_at(-step)})
        own = own + anc_far[n].astype(jnp.float32)
    loads[4].wait()
    anc_all[span(row, anc_rows), :] = (rhs_anc[...] - own).astype(jnp.bfloat16)
    gather_anc = DirectGather(copies, place, lambda r: anc_all.at[span(r, anc_rows), :])
    gather_anc.start()
    for t in (4, 5):
        reduce_step(t)
    gather_anc.finish()
    loads[6].wait()
    anc_sol_all[span(row, anc_rows), :] = dot(dinv_anc[...], anc_all[...]).astype(jnp.bfloat16)
    gather_out = DirectGather(copies, place, lambda r: anc_sol_all.at[span(r, anc_rows), :])
    gather_out.start()
    store_anc = pltpu.make_async_copy(
        anc_sol_all.at[span(row, anc_rows), :], anc_out, local_sem.at[9]
    )
    store_anc.start()
    for t in range(6, ups):
        reduce_step(t)
    loads[5].wait()
    slot = slot_of(layer)
    for p in range(PIECES):
        piece = pl.ds(p * cut, cut)
        copies.arrived(up[ups - 1, p], up_in.at[ups - 1, piece, :], {"layer": layer_at(-1)})
        copies.arrived(down[downs - 1, p], down_in.at[downs - 1, piece, :], {"layer": layer_at(1)})
        summed = partial[slot, piece, :] + up_in[ups - 1, piece, :].astype(jnp.float32)
        summed = summed + down_in[downs - 1, piece, :].astype(jnp.float32)
        result[piece, :] = rhs_high[piece, :] - summed
    gather_out.finish()
    loads[7].wait()
    result[...] = result[...] - dot(lower[...], anc_sol_all[...])
    store_high = pltpu.make_async_copy(result, high_out, local_sem.at[10])
    store_high.start()
    copies.drain()
    store_sol.wait()
    store_anc.wait()
    store_high.wait()


def on_device(layers, rhs_local, dinv_local, lower_anc, lower_high, row_blocks, rhs_anc, rhs_high, dinv_anc, lower_anc_high):
    supers, rows, width = rhs_local.shape[1:]
    order = dinv_local.shape[3]
    anc_rows, anc_order = dinv_anc.shape
    held = supers * row_blocks.shape[2]
    bf16, f32 = jnp.bfloat16, jnp.float32
    anywhere = pl.BlockSpec(memory_space=pl.ANY)
    half = layers // 2
    return pl.pallas_call(
        functools.partial(kernel, layers),
        out_shape=(
            jax.ShapeDtypeStruct(rhs_local.shape, bf16),
            jax.ShapeDtypeStruct(rhs_anc.shape, bf16),
            jax.ShapeDtypeStruct(rhs_high.shape, f32),
        ),
        in_specs=[pl.BlockSpec(memory_space=pltpu.SMEM)] + [anywhere] * 8,
        out_specs=(anywhere,) * 3,
        scratch_shapes=[
            pltpu.VMEM(dinv_local.shape[1:], bf16),
            pltpu.VMEM(lower_anc.shape[1:], bf16),
            pltpu.VMEM(lower_high.shape[1:], bf16),
            pltpu.VMEM(rhs_anc.shape, f32),
            pltpu.VMEM(rhs_high.shape, f32),
            pltpu.VMEM(dinv_anc.shape, bf16),
            pltpu.VMEM(lower_anc_high.shape, bf16),
            pltpu.VMEM((supers, order, width), bf16),
            pltpu.VMEM((supers, order, width), bf16),
            pltpu.VMEM((anc_order, width), bf16),
            pltpu.VMEM((anc_order, width), bf16),
            pltpu.VMEM((held + 1, BLOCK, width), f32),
            pltpu.VMEM((lower_high.shape[2], width), f32),
            pltpu.VMEM((half, BLOCK, width), bf16),
            pltpu.VMEM((half, BLOCK, width), bf16),
            pltpu.VMEM((half, BLOCK, width), bf16),
            pltpu.VMEM((half, BLOCK, width), bf16),
            pltpu.VMEM((3, anc_rows, width), bf16),
            pltpu.VMEM((3, anc_rows, width), bf16),
            pltpu.VMEM((2, anc_rows, width), bf16),
            pltpu.VMEM(rhs_high.shape, f32),
            pltpu.SMEM((held,), jnp.int32),
            pltpu.SemaphoreType.DMA((256,)),
            pltpu.SemaphoreType.DMA((256,)),
            pltpu.SemaphoreType.DMA((11,)),
        ],
        compiler_params=pltpu.CompilerParams(collective_id=0, has_side_effects=True),
    )(row_blocks, rhs_local, dinv_local, lower_anc, lower_high, rhs_anc, rhs_high, dinv_anc, lower_anc_high)


def solution(mesh):
    return jax.shard_map(
        functools.partial(on_device, mesh.shape["layer"]),
        mesh=mesh,
        in_specs=(
            P("layer", None, "row", None),
            P("layer", None, "row", None),
            P("layer", None, "row", None),
            P("layer", None, "row", None),
            P("layer", None, "row"),
            P("row", None),
            P(("row", "layer"), None),
            P("row", None),
            P(("row", "layer"), None),
        ),
        out_specs=(P("layer", None, "row", None), P("row", None), P(("row", "layer"), None)),
        check_vma=False,
    )
```

time: 159 us -> 77.5 us (0.49); the launches traced: 156 us -> 77.2 us
  blocking collectives: 101 us -> 0 us
  Pallas kernels: 0 us -> 72.3 us
  starting transfers between devices: 13.8 us -> 0 us
  between operations: 14.2 us -> 0.64 us
  waiting for transfers between devices: 12.5 us -> 0 us
  matrix products: 7.46 us -> 0 us
  local copies, waits for them, and re-layouts: 7.86 us -> 4.26 us
    pallas_call x0 -> x1, Pallas kernels: none -> 72.3 us  [on_device(): pl.pallas_call(functools.partial(kernel, layers), out_shape=(jax.ShapeDty...]
    all_gather x2 -> x0, blocking collectives: 53.3 us -> none  [the longest x1 29.8 us: on_device(): lax.all_gather(anc_rhs, 'row', axis=0, tiled=True)]
    all_to_all x2 -> x0, blocking collectives: 47.4 us -> none  [copy_for_each(): lax.all_to_all(jnp.broadcast_to(shard[None], (count, *shard.shape)), axis...]
    all_to_all x1 -> x0, starting transfers between devices: 13.7 us -> none  [copy_for_each(): lax.all_to_all(jnp.broadcast_to(shard[None], (count, *shard.shape)), axis...]
    all_to_all x1 -> x0, waiting for transfers between devices: 12.5 us -> none  [copy_for_each(): lax.all_to_all(jnp.broadcast_to(shard[None], (count, *shard.shape)), axis...]
    dot_general x6 -> x0, matrix products: 7.46 us -> none  [the longest x1 3.59 us: on_device(): jnp.einsum('sik,skc->sic', high_mine, portion, preferred_element_type=jnp...]
    reshape x1 -> x0, local copies, waits for them, and re-layouts: 2.15 us -> none  [on_device(): high_blocks = high_next.reshape(supers, blocks_held, BLOCK, width)]
    unnamed x22 -> x3, local copies, waits for them, and re-layouts: 2.33 us -> 4.26 us
  transfers between devices with their start and end apart: 2 -> 0, of which waited for: 1 -> 0; matrix products, arithmetic and copies ran while one was open for 7% -> 0% of each run, Pallas kernels for 0% -> 0%
where the time goes in v1:
time: 77.5 us; the launch traced here: 77.2 us
  Pallas kernels  72.3 us (93%)
  local copies, waits for them, and re-layouts  4.26 us (5%)
    pallas_call x1, Pallas kernels, on_device(): pl.pallas_call(functools.partial(kernel, layers), out_shape=(jax.ShapeDty...  72.3 us
    unnamed x3, local copies, waits for them, and re-layouts  4.26 us

profile of v1, /device:TPU:1, one launch (start us, length us, event | category | flops | bytes accessed | tf_op | source)
XLA Modules:
  0.0 77.2 jit_solution(11225460151038866351)
XLA Ops:
  0.6 72.3 %shard_map.112 = (bf16[1,2,32,256]{3,2,1,0:T(8,128)(2,1)}, bf16[32,256]{1,0:T(8,128)(2,1)}, f32[128,256]{1,0:T(8,128)}) custom-call(s32[1,2,8]{2,1,0:T(2,128)} %blocks_ref.1, bf16[1,2,32,256]{3,2,1,0:T(8,128)(2,1)} %rhs_hbm.1, bf16[1,2,32,1024]{3,2,1,0:T(8,128)(2,1)} %dinv_hbm.1, bf16[1,2,32,1024]{3,2,1,0:T(8,128)(2,1)} %anc_hbm.1, ...), custom_call_target="tpu_custom_call" | custom-call | tf_op jit(solution)/shard_map/pallas_call | solution.py:405
  72.9 1.4 %copy.15 = bf16[1,2,32,256]{3,2,1,0:T(8,128)(2,1)} copy(bf16[1,2,32,256]{3,2,1,0:T(8,128)(2,1)} %get-tuple-element.6) | data formatting | bytes 65536
  74.3 1.3 %copy.16 = bf16[32,256]{1,0:T(8,128)(2,1)} copy(bf16[32,256]{1,0:T(8,128)(2,1)} %get-tuple-element.7) | data formatting | bytes 32768
  75.6 1.6 %copy.17 = f32[128,256]{1,0:T(8,128)} copy(f32[128,256]{1,0:T(8,128)} %get-tuple-element.8) | data formatting | bytes 262144

commit v2 on v1

--- a/solution.py
+++ b/solution.py
@@ -11,8 +11,7 @@
 HBLK = 16
 X, Y, CORES = 4, 4, 2
 NEAR_FIRST = (1, 3, 2)
-PIECES = 4
-STOP = 99
+PIECES = 2
 
 
 class Copies:
@@ -192,18 +191,19 @@
     high,
     rhs_anc,
     rhs_high,
-    dinv_anc,
+    dinv_anc_all,
     lower,
     rhs_all,
     sol_all,
     anc_all,
-    anc_sol_all,
+    anc_sol,
     partial,
     product,
-    up_in,
-    up_out,
-    down_in,
-    down_out,
+    reach,
+    chain_in,
+    chain_out,
+    side_in,
+    side_out,
     anc_near,
     anc_far,
     anc_own,
@@ -212,6 +212,7 @@
     send_sem,
     recv_sem,
     local_sem,
+    relay,
 ):
     place = Place()
     row = place.row
@@ -223,6 +224,9 @@
 
     def layer_at(step):
         return lax.rem(layer + (step + layers), layers)
+
+    def signal(sem, where):
+        pl.semaphore_signal(sem, inc=1, device_id=where, device_id_type=pl.DeviceIdType.MESH)
 
     def span(r, count):
         return pl.ds(pl.multiple_of(r * count, count), count)
@@ -242,7 +246,7 @@
             (high_hbm.at[0], high),
             (rhs_anc_hbm, rhs_anc),
             (rhs_high_hbm, rhs_high),
-            (dinv_anc_hbm, dinv_anc),
+            (dinv_anc_hbm, dinv_anc_all.at[span(row, anc_rows), :]),
             (lower_hbm, lower),
         )
     ):
@@ -252,18 +256,12 @@
 
     barrier = pltpu.get_barrier_semaphore()
     plane = [(dx, dy) for dx in range(X) for dy in range(Y) if dx or dy]
-    along = [1, -1, 2, -2, 4, -4, 8]
+    along = [1, -1, 2, -2]
+    for step in along:
+        signal(barrier, {"layer": layer_at(step)})
     for dx, dy in plane:
-        pl.semaphore_signal(
-            barrier, inc=1, device_id={"row": place.at(dx, dy)}, device_id_type=pl.DeviceIdType.MESH
-        )
-    pl.semaphore_signal(
-        barrier, inc=1, device_id={"row": place.at(0, 0, True)}, device_id_type=pl.DeviceIdType.MESH
-    )
-    for step in along:
-        pl.semaphore_signal(
-            barrier, inc=1, device_id={"layer": layer_at(step)}, device_id_type=pl.DeviceIdType.MESH
-        )
+        signal(barrier, {"row": place.at(dx, dy)})
+    signal(barrier, {"row": place.at(0, 0, True)})
 
     home = [blocks_ref[0, i // (held // supers), i % (held // supers)] for i in range(held)]
     for i in range(held):
@@ -275,10 +273,14 @@
 
     loads[0].wait()
     pl.semaphore_wait(barrier, len(plane) + 1 + len(along))
+    for step in (2, -2):
+        signal(relay.at[0], {"layer": layer_at(step)})
 
     gather_rhs = TreeGather(copies, place, half_of(rhs_all), both_of(rhs_all))
     gather_rhs.start()
     gather_rhs.finish()
+    pl.semaphore_wait(relay.at[0], 2)
+    signal(relay.at[1], {"layer": layer_at(-4)})
     loads[1].wait()
     for s in range(supers):
         sol_all[s, span(row, rows), :] = dot(dinv[s], rhs_all[s]).astype(jnp.bfloat16)
@@ -289,6 +291,7 @@
     )
     store_sol.start()
     gather_sol.finish()
+    pl.semaphore_wait(relay.at[1], 1)
 
     loads[2].wait()
     own = dot(anc[0], sol_all[0])
@@ -298,6 +301,9 @@
     near = {step: copies.take() for step in (1, -1, -2)}
     for n, step in enumerate(near):
         copies.start(near[step], anc_own.at[0], anc_near.at[n], {"layer": layer_at(step)})
+    loads[6].wait()
+    gather_dinv = DirectGather(copies, place, lambda r: dinv_anc_all.at[span(r, anc_rows), :])
+    gather_dinv.start()
 
     loads[3].wait()
     for s in range(supers):
@@ -313,35 +319,51 @@
         return last
 
     cut = BLOCK // PIECES
-    ups, downs = layers // 2, layers // 2 - 1
-    up = {(t, p): copies.take() for t in range(ups) for p in range(PIECES)}
-    down = {(t, p): copies.take() for t in range(downs) for p in range(PIECES)}
-
-    def reduce_step(t):
-        lanes = []
-        if t < ups:
-            lanes.append((up, up_in, up_out, 1, layer_at(ups - t)))
-        if t < downs:
-            lanes.append((down, down_in, down_out, -1, layer_at(t - downs)))
-        slots = [slot_of(h) for *_, h in lanes]
+    ways = (1, -1)
+    far_half = {1: range(0, PIECES // 2), -1: range(PIECES // 2, PIECES)}
+    chain = {(w, d, p): copies.take() for w in ways for d in (8, 6, 4, 2) for p in range(PIECES)}
+    side = {(w, d): copies.take() for w in ways for d in (7, 5, 3, 1)}
+
+    def box(w, n):
+        return n if w == 1 else n + 4
+
+    def send_chain(w, d, p, value):
+        piece = pl.ds(p * cut, cut)
+        at = box(w, d // 2 - 1)
+        chain_out[at, piece, :] = value.astype(jnp.bfloat16)
+        copies.start(
+            chain[w, d, p],
+            chain_out.at[at, piece, :],
+            chain_in.at[at, piece, :],
+            {"layer": layer_at(2 * w)},
+        )
+
+    def send_sides(d):
+        for w in ways:
+            at = box(w, d // 2)
+            side_out[at] = partial[slot_of(layer_at(w * d))].astype(jnp.bfloat16)
+            copies.start(side[w, d], side_out.at[at], side_in.at[at], {"layer": layer_at(w)})
+
+    def arrived(w, d, p, value, fresh):
+        piece = pl.ds(p * cut, cut)
+        if d + 2 < 8 or p in far_half[w]:
+            at = box(w, d // 2)
+            copies.arrived(
+                chain[w, d + 2, p], chain_in.at[at, piece, :], {"layer": layer_at(-2 * w)}
+            )
+            value = value + chain_in[at, piece, :].astype(jnp.float32)
+        at = box(w, d // 2)
+        if fresh:
+            copies.arrived(side[w, d + 1], side_in.at[at], {"layer": layer_at(-w)})
+        return value + side_in[at, piece, :].astype(jnp.float32)
+
+    def pass_on(d):
+        slots = {w: slot_of(layer_at(w * d)) for w in ways}
         for p in range(PIECES):
             piece = pl.ds(p * cut, cut)
-            for (index, inbox, outbox, step, _), slot in zip(lanes, slots):
-                value = partial[slot, piece, :]
-                if t:
-                    copies.arrived(
-                        index[t - 1, p], inbox.at[t - 1, piece, :], {"layer": layer_at(-step)}
-                    )
-                    value = value + inbox[t - 1, piece, :].astype(jnp.float32)
-                outbox[t, piece, :] = value.astype(jnp.bfloat16)
-                copies.start(
-                    index[t, p],
-                    outbox.at[t, piece, :],
-                    inbox.at[t, piece, :],
-                    {"layer": layer_at(step)},
-                )
-
-    reduce_step(0)
+            for w in ways:
+                value = arrived(w, d, p, partial[slots[w], piece, :], p == 0)
+                send_chain(w, d, p, value)
 
     for n, step in enumerate(near):
         copies.arrived(near[step], anc_near.at[n], {"layer": layer_at(-step)})
@@ -351,8 +373,14 @@
     for n, step in enumerate(far):
         copies.start(far[step], anc_own.at[1], anc_far.at[n], {"layer": layer_at(step)})
 
-    for t in (1, 2, 3):
-        reduce_step(t)
+    slot = slot_of(layer_at(8))
+    for w in ways:
+        for p in far_half[w]:
+            send_chain(w, 8, p, partial[slot, pl.ds(p * cut, cut), :])
+    send_sides(7)
+    send_sides(5)
+    pass_on(6)
+    send_sides(3)
 
     for n, step in enumerate(far):
         copies.arrived(far[step], anc_far.at[n], {"layer": layer_at(-step)})
@@ -361,37 +389,48 @@
     anc_all[span(row, anc_rows), :] = (rhs_anc[...] - own).astype(jnp.bfloat16)
     gather_anc = DirectGather(copies, place, lambda r: anc_all.at[span(r, anc_rows), :])
     gather_anc.start()
-    for t in (4, 5):
-        reduce_step(t)
+    pass_on(4)
+    send_sides(1)
+    gather_dinv.finish()
+    loads[7].wait()
+    spread = dot(lower[...], dinv_anc_all[...])
+    reach[0] = spread.astype(jnp.bfloat16)
+    reach[1] = (spread - reach[0].astype(jnp.float32)).astype(jnp.bfloat16)
+    pass_on(2)
     gather_anc.finish()
-    loads[6].wait()
-    anc_sol_all[span(row, anc_rows), :] = dot(dinv_anc[...], anc_all[...]).astype(jnp.bfloat16)
-    gather_out = DirectGather(copies, place, lambda r: anc_sol_all.at[span(r, anc_rows), :])
-    gather_out.start()
-    store_anc = pltpu.make_async_copy(
-        anc_sol_all.at[span(row, anc_rows), :], anc_out, local_sem.at[9]
-    )
+    anc_sol[...] = dot(dinv_anc_all[span(row, anc_rows), :], anc_all[...]).astype(jnp.bfloat16)
+    store_anc = pltpu.make_async_copy(anc_sol, anc_out, local_sem.at[9])
     store_anc.start()
-    for t in range(6, ups):
-        reduce_step(t)
     loads[5].wait()
+    result[...] = rhs_high[...] - dot(reach[0], anc_all[...]) - dot(reach[1], anc_all[...])
     slot = slot_of(layer)
     for p in range(PIECES):
         piece = pl.ds(p * cut, cut)
-        copies.arrived(up[ups - 1, p], up_in.at[ups - 1, piece, :], {"layer": layer_at(-1)})
-        copies.arrived(down[downs - 1, p], down_in.at[downs - 1, piece, :], {"layer": layer_at(1)})
-        summed = partial[slot, piece, :] + up_in[ups - 1, piece, :].astype(jnp.float32)
-        summed = summed + down_in[downs - 1, piece, :].astype(jnp.float32)
-        result[piece, :] = rhs_high[piece, :] - summed
-    gather_out.finish()
-    loads[7].wait()
-    result[...] = result[...] - dot(lower[...], anc_sol_all[...])
+        summed = partial[slot, piece, :]
+        for w in ways:
+            summed = arrived(w, 0, p, summed, p == 0)
+        result[piece, :] = result[piece, :] - summed
     store_high = pltpu.make_async_copy(result, high_out, local_sem.at[10])
     store_high.start()
     copies.drain()
     store_sol.wait()
     store_anc.wait()
     store_high.wait()
+
+
+def hand_over(*refs):
+    count = len(refs) // 3
+    given, wanted, held = refs[:count], refs[count : 2 * count], refs[2 * count : -1]
+    sem = refs[-1]
+    loads = [pltpu.make_async_copy(a, b, sem.at[0, n]) for n, (a, b) in enumerate(zip(given, held))]
+    stores = [pltpu.make_async_copy(a, b, sem.at[1, n]) for n, (a, b) in enumerate(zip(held, wanted))]
+    for load in loads:
+        load.start()
+    for load, store in zip(loads, stores):
+        load.wait()
+        store.start()
+    for store in stores:
+        store.wait()
 
 
 def on_device(layers, rhs_local, dinv_local, lower_anc, lower_high, row_blocks, rhs_anc, rhs_high, dinv_anc, lower_anc_high):
@@ -401,14 +440,14 @@
     held = supers * row_blocks.shape[2]
     bf16, f32 = jnp.bfloat16, jnp.float32
     anywhere = pl.BlockSpec(memory_space=pl.ANY)
-    half = layers // 2
-    return pl.pallas_call(
+    shapes = (
+        jax.ShapeDtypeStruct(rhs_local.shape, bf16),
+        jax.ShapeDtypeStruct(rhs_anc.shape, bf16),
+        jax.ShapeDtypeStruct(rhs_high.shape, f32),
+    )
+    outs = pl.pallas_call(
         functools.partial(kernel, layers),
-        out_shape=(
-            jax.ShapeDtypeStruct(rhs_local.shape, bf16),
-            jax.ShapeDtypeStruct(rhs_anc.shape, bf16),
-            jax.ShapeDtypeStruct(rhs_high.shape, f32),
-        ),
+        out_shape=shapes,
         in_specs=[pl.BlockSpec(memory_space=pltpu.SMEM)] + [anywhere] * 8,
         out_specs=(anywhere,) * 3,
         scratch_shapes=[
@@ -417,18 +456,19 @@
             pltpu.VMEM(lower_high.shape[1:], bf16),
             pltpu.VMEM(rhs_anc.shape, f32),
             pltpu.VMEM(rhs_high.shape, f32),
-            pltpu.VMEM(dinv_anc.shape, bf16),
+            pltpu.VMEM((anc_order, anc_order), bf16),
             pltpu.VMEM(lower_anc_high.shape, bf16),
             pltpu.VMEM((supers, order, width), bf16),
             pltpu.VMEM((supers, order, width), bf16),
             pltpu.VMEM((anc_order, width), bf16),
-            pltpu.VMEM((anc_order, width), bf16),
+            pltpu.VMEM((anc_rows, width), bf16),
             pltpu.VMEM((held + 1, BLOCK, width), f32),
             pltpu.VMEM((lower_high.shape[2], width), f32),
-            pltpu.VMEM((half, BLOCK, width), bf16),
-            pltpu.VMEM((half, BLOCK, width), bf16),
-            pltpu.VMEM((half, BLOCK, width), bf16),
-            pltpu.VMEM((half, BLOCK, width), bf16),
+            pltpu.VMEM((2, BLOCK, anc_order), bf16),
+            pltpu.VMEM((8, BLOCK, width), bf16),
+            pltpu.VMEM((8, BLOCK, width), bf16),
+            pltpu.VMEM((8, BLOCK, width), bf16),
+            pltpu.VMEM((8, BLOCK, width), bf16),
             pltpu.VMEM((3, anc_rows, width), bf16),
             pltpu.VMEM((3, anc_rows, width), bf16),
             pltpu.VMEM((2, anc_rows, width), bf16),
@@ -437,9 +477,18 @@
             pltpu.SemaphoreType.DMA((256,)),
             pltpu.SemaphoreType.DMA((256,)),
             pltpu.SemaphoreType.DMA((11,)),
+            pltpu.SemaphoreType.REGULAR((2,)),
         ],
         compiler_params=pltpu.CompilerParams(collective_id=0, has_side_effects=True),
     )(row_blocks, rhs_local, dinv_local, lower_anc, lower_high, rhs_anc, rhs_high, dinv_anc, lower_anc_high)
+    return pl.pallas_call(
+        hand_over,
+        out_shape=shapes,
+        in_specs=[anywhere] * 3,
+        out_specs=(anywhere,) * 3,
+        scratch_shapes=[pltpu.VMEM(a.shape, a.dtype) for a in shapes]
+        + [pltpu.SemaphoreType.DMA((2, 3))],
+    )(*outs)
 
 
 def solution(mesh):

time: 77.5 us -> 65.9 us (0.85)
  Pallas kernels: 72.3 us -> 64.6 us
  local copies, waits for them, and re-layouts: 4.26 us -> 0 us
    pallas_call x1 -> x2, Pallas kernels: 72.3 us -> 64.6 us  [the longest x1 62.9 us: on_device(): pl.pallas_call(functools.partial(kernel, layers), out_shape=shapes, in_sp...]
    unnamed x3 -> x0, local copies, waits for them, and re-layouts: 4.26 us -> none
where the time goes in v2:
time: 65.9 us; the launch traced here: 65.2 us
  Pallas kernels  64.6 us (98%)
    pallas_call x1, Pallas kernels, on_device(): pl.pallas_call(functools.partial(kernel, layers), out_shape=shapes, in_sp...  62.9 us
    pallas_call x1, Pallas kernels, on_device(): pl.pallas_call(hand_over, out_shape=shapes, in_specs=[anywhere] * 3, out_...  1.65 us

profile of v2, /device:TPU:1, one launch (start us, length us, event | category | flops | bytes accessed | tf_op | source)
XLA Modules:
  0.0 65.2 jit_solution(17554458054931064606)
XLA Ops:
  0.6 62.9 %shard_map.112 = (bf16[1,2,32,256]{3,2,1,0:T(8,128)(2,1)}, bf16[32,256]{1,0:T(8,128)(2,1)}, f32[128,256]{1,0:T(8,128)}) custom-call(s32[1,2,8]{2,1,0:T(2,128)} %blocks_ref.1, bf16[1,2,32,256]{3,2,1,0:T(8,128)(2,1)} %rhs_hbm.1, bf16[1,2,32,1024]{3,2,1,0:T(8,128)(2,1)} %dinv_hbm.1, bf16[1,2,32,1024]{3,2,1,0:T(8,128)(2,1)} %anc_hbm.1, ...), custom_call_target="tpu_custom_call" | custom-call | tf_op jit(solution)/shard_map/pallas_call | solution.py:448
  63.6 1.6 %shard_map.113 = (bf16[1,2,32,256]{3,2,1,0:T(8,128)(2,1)}, bf16[32,256]{1,0:T(8,128)(2,1)}, f32[128,256]{1,0:T(8,128)}) custom-call(bf16[1,2,32,256]{3,2,1,0:T(8,128)(2,1)} %get-tuple-element.6.refs_0_, bf16[32,256]{1,0:T(8,128)(2,1)} %get-tuple-element.7.refs_1_, f32[128,256]{1,0:T(8,128)} %get-tuple-element.8.refs_2_), custom_call_target="tpu_custom_call" | custom-call | tf_op jit(solution)/shard_map/pallas_call | solution.py:484

commit v3 on v2

--- a/solution.py
+++ b/solution.py
@@ -10,7 +10,6 @@
 BLOCK = 128
 HBLK = 16
 X, Y, CORES = 4, 4, 2
-NEAR_FIRST = (1, 3, 2)
 PIECES = 2
 
 
@@ -71,6 +70,8 @@
 class TreeGather:
     def __init__(self, copies, place, half, both):
         self.copies, self.place, self.half, self.both = copies, place, half, both
+        self.order = [(dx, dy) for dx in range(X) for dy in range(Y) if dx or dy]
+        self.order.sort(key=lambda p: (min(p[0], X - p[0]) + min(p[1], Y - p[1]), p))
         self.first = {(h, d): copies.take() for h in (0, 1) for d in (1, 2, 3)}
         self.second = {
             (h, e, d): copies.take() for h in (0, 1) for e in range(4) for d in (1, 2, 3)
@@ -88,7 +89,7 @@
     def send_second(self, h, e):
         at = self.place.at
         shard = self.half(h, at(*self.along(h, -e, 0)))
-        for d in NEAR_FIRST:
+        for d in (1, 3, 2):
             self.copies.start(
                 self.second[h, e, d], shard, shard, {"row": at(*self.along(h, 0, d))}
             )
@@ -99,16 +100,16 @@
         self.copies.start(self.other[dx, dy], shard, shard, {"row": at(0, 0, True)})
 
     def start(self):
-        for d in NEAR_FIRST:
+        for d in (1, 3, 2):
             for h in (0, 1):
                 self.send_first(h, d)
         for h in (0, 1):
             self.send_second(h, 0)
         self.send_other(0, 0)
 
-    def finish(self):
-        at = self.place.at
-        for e in NEAR_FIRST:
+    def turn(self):
+        at = self.place.at
+        for e in (1, 3, 2):
             for h in (0, 1):
                 self.copies.arrived(
                     self.first[h, e],
@@ -116,9 +117,10 @@
                     {"row": at(*self.along(h, -e, 0))},
                 )
                 self.send_second(h, e)
-        order = [(dx, dy) for dx in range(X) for dy in range(Y) if dx or dy]
-        order.sort(key=lambda p: (min(p[0], X - p[0]) + min(p[1], Y - p[1]), p))
-        for dx, dy in order:
+
+    def forward(self):
+        at = self.place.at
+        for dx, dy in self.order:
             source = at(-dx, -dy)
             if dy:
                 self.copies.arrived(
@@ -129,7 +131,10 @@
                     self.second[1, dy, dx], self.half(1, source), {"row": at(-dx, 0)}
                 )
             self.send_other(dx, dy)
-        for dx, dy in [(0, 0)] + order:
+
+    def complete(self):
+        at = self.place.at
+        for dx, dy in [(0, 0)] + self.order:
             self.copies.arrived(
                 self.other[dx, dy], self.both(at(-dx, -dy, True)), {"row": at(0, 0, True)}
             )
@@ -155,13 +160,16 @@
         shard = self.shard(at(-dx, -dy))
         self.copies.start(self.other[dx, dy], shard, shard, {"row": at(0, 0, True)})
 
-    def finish(self):
+    def forward(self):
         at = self.place.at
         for dx, dy in self.order:
             self.copies.arrived(
                 self.peer[dx, dy], self.shard(at(-dx, -dy)), {"row": at(-dx, -dy)}
             )
             self.send_other(dx, dy)
+
+    def complete(self):
+        at = self.place.at
         for dx, dy in [(0, 0)] + self.order:
             self.copies.arrived(
                 self.other[dx, dy], self.shard(at(-dx, -dy, True)), {"row": at(0, 0, True)}
@@ -174,7 +182,7 @@
 
 def kernel(
     layers,
-    blocks_ref,
+    blocks_hbm,
     rhs_hbm,
     dinv_hbm,
     anc_hbm,
@@ -208,7 +216,9 @@
     anc_far,
     anc_own,
     result,
+    blocks_ref,
     before,
+    final,
     send_sem,
     recv_sem,
     local_sem,
@@ -231,11 +241,8 @@
     def span(r, count):
         return pl.ds(pl.multiple_of(r * count, count), count)
 
-    def half_of(ref):
-        return lambda h, r: ref.at[h, span(r, rows), :]
-
-    def both_of(ref):
-        return lambda r: ref.at[:, span(r, rows), :]
+    def shards_of(ref, s):
+        return lambda r: ref.at[s, span(r, rows), :]
 
     loads = []
     for n, (src, dst) in enumerate(
@@ -248,6 +255,7 @@
             (rhs_high_hbm, rhs_high),
             (dinv_anc_hbm, dinv_anc_all.at[span(row, anc_rows), :]),
             (lower_hbm, lower),
+            (blocks_hbm, blocks_ref),
         )
     ):
         load = pltpu.make_async_copy(src, dst, local_sem.at[n])
@@ -255,68 +263,83 @@
         loads.append(load)
 
     barrier = pltpu.get_barrier_semaphore()
-    plane = [(dx, dy) for dx in range(X) for dy in range(Y) if dx or dy]
+    lines = [(d, 0) for d in (2, 1, 3)] + [(0, d) for d in (2, 1, 3)]
     along = [1, -1, 2, -2]
     for step in along:
         signal(barrier, {"layer": layer_at(step)})
-    for dx, dy in plane:
+    for dx, dy in lines:
         signal(barrier, {"row": place.at(dx, dy)})
     signal(barrier, {"row": place.at(0, 0, True)})
 
+    loads[0].wait()
+    pl.semaphore_wait(barrier, len(lines) + 1 + len(along))
+    for step in (2, -2):
+        signal(relay.at[0], {"layer": layer_at(step)})
+
+    gather_rhs = TreeGather(
+        copies,
+        place,
+        lambda h, r: rhs_all.at[h, span(r, rows), :],
+        lambda r: rhs_all.at[:, span(r, rows), :],
+    )
+    gather_rhs.start()
+    loads[8].wait()
     home = [blocks_ref[0, i // (held // supers), i % (held // supers)] for i in range(held)]
     for i in range(held):
         last = jnp.int32(held)
         for j in range(i):
             last = jnp.where(home[j] == home[i], j, last)
         before[i] = last
+    for h in range(HBLK):
+        last = jnp.int32(held)
+        for i in range(held):
+            last = jnp.where(home[i] == h, i, last)
+        final[h] = last
     partial[held] = jnp.zeros_like(partial[held])
 
-    loads[0].wait()
-    pl.semaphore_wait(barrier, len(plane) + 1 + len(along))
-    for step in (2, -2):
-        signal(relay.at[0], {"layer": layer_at(step)})
-
-    gather_rhs = TreeGather(copies, place, half_of(rhs_all), both_of(rhs_all))
-    gather_rhs.start()
-    gather_rhs.finish()
-    pl.semaphore_wait(relay.at[0], 2)
-    signal(relay.at[1], {"layer": layer_at(-4)})
+    gather_sol = [DirectGather(copies, place, shards_of(sol_all, s)) for s in range(supers)]
+    store_sol = []
+    gather_rhs.turn()
+    gather_rhs.forward()
+    gather_rhs.complete()
     loads[1].wait()
     for s in range(supers):
         sol_all[s, span(row, rows), :] = dot(dinv[s], rhs_all[s]).astype(jnp.bfloat16)
-    gather_sol = TreeGather(copies, place, half_of(sol_all), both_of(sol_all))
-    gather_sol.start()
+        gather_sol[s].start()
+    pl.semaphore_wait(relay.at[0], 2)
+    signal(relay.at[1], {"layer": layer_at(-4)})
     store_sol = pltpu.make_async_copy(
-        sol_all.at[:, span(row, rows), :], sol_out.at[0], local_sem.at[8]
+        sol_all.at[:, span(row, rows), :], sol_out.at[0], local_sem.at[11]
     )
     store_sol.start()
-    gather_sol.finish()
-    pl.semaphore_wait(relay.at[1], 1)
-
+
+    near = {step: copies.take() for step in (1, -1, -2)}
     loads[2].wait()
-    own = dot(anc[0], sol_all[0])
-    for s in range(1, supers):
-        own += dot(anc[s], sol_all[s])
-    anc_own[0] = own.astype(jnp.bfloat16)
-    near = {step: copies.take() for step in (1, -1, -2)}
-    for n, step in enumerate(near):
-        copies.start(near[step], anc_own.at[0], anc_near.at[n], {"layer": layer_at(step)})
-    loads[6].wait()
-    gather_dinv = DirectGather(copies, place, lambda r: dinv_anc_all.at[span(r, anc_rows), :])
-    gather_dinv.start()
-
     loads[3].wait()
+    own = None
     for s in range(supers):
+        gather_sol[s].forward()
+        gather_sol[s].complete()
+        term = dot(anc[s], sol_all[s])
+        own = term if own is None else own + term
+        if s == supers - 1:
+            anc_own[0] = own.astype(jnp.bfloat16)
+            for n, step in enumerate(near):
+                copies.start(near[step], anc_own.at[0], anc_near.at[n], {"layer": layer_at(step)})
+            loads[6].wait()
+            gather_dinv = TreeGather(
+                copies,
+                place,
+                lambda h, r: dinv_anc_all.at[
+                    pl.ds(pl.multiple_of(r * anc_rows + h * (anc_rows // 2), anc_rows // 2), anc_rows // 2), :
+                ],
+                lambda r: dinv_anc_all.at[span(r, anc_rows), :],
+            )
+            gather_dinv.start()
         product[...] = dot(high[s], sol_all[s])
         for q in range(held // supers):
             i = s * (held // supers) + q
             partial[i] = product[q * BLOCK : (q + 1) * BLOCK, :] + partial[before[i]]
-
-    def slot_of(h):
-        last = jnp.int32(held)
-        for i in range(held):
-            last = jnp.where(home[i] == h, i, last)
-        return last
 
     cut = BLOCK // PIECES
     ways = (1, -1)
@@ -341,7 +364,7 @@
     def send_sides(d):
         for w in ways:
             at = box(w, d // 2)
-            side_out[at] = partial[slot_of(layer_at(w * d))].astype(jnp.bfloat16)
+            side_out[at] = partial[final[layer_at(w * d)]].astype(jnp.bfloat16)
             copies.start(side[w, d], side_out.at[at], side_in.at[at], {"layer": layer_at(w)})
 
     def arrived(w, d, p, value, fresh):
@@ -358,13 +381,19 @@
         return value + side_in[at, piece, :].astype(jnp.float32)
 
     def pass_on(d):
-        slots = {w: slot_of(layer_at(w * d)) for w in ways}
+        slots = {w: final[layer_at(w * d)] for w in ways}
         for p in range(PIECES):
             piece = pl.ds(p * cut, cut)
             for w in ways:
                 value = arrived(w, d, p, partial[slots[w], piece, :], p == 0)
                 send_chain(w, d, p, value)
 
+    slot = final[layer_at(8)]
+    for w in ways:
+        for p in far_half[w]:
+            send_chain(w, 8, p, partial[slot, pl.ds(p * cut, cut), :])
+    send_sides(7)
+    pl.semaphore_wait(relay.at[1], 1)
     for n, step in enumerate(near):
         copies.arrived(near[step], anc_near.at[n], {"layer": layer_at(-step)})
         own = own + anc_near[n].astype(jnp.float32)
@@ -372,16 +401,13 @@
     far = {step: copies.take() for step in (8, 4, -4)}
     for n, step in enumerate(far):
         copies.start(far[step], anc_own.at[1], anc_far.at[n], {"layer": layer_at(step)})
-
-    slot = slot_of(layer_at(8))
-    for w in ways:
-        for p in far_half[w]:
-            send_chain(w, 8, p, partial[slot, pl.ds(p * cut, cut), :])
-    send_sides(7)
     send_sides(5)
+    gather_dinv.turn()
     pass_on(6)
     send_sides(3)
-
+    gather_dinv.forward()
+    pass_on(4)
+    send_sides(1)
     for n, step in enumerate(far):
         copies.arrived(far[step], anc_far.at[n], {"layer": layer_at(-step)})
         own = own + anc_far[n].astype(jnp.float32)
@@ -389,21 +415,20 @@
     anc_all[span(row, anc_rows), :] = (rhs_anc[...] - own).astype(jnp.bfloat16)
     gather_anc = DirectGather(copies, place, lambda r: anc_all.at[span(r, anc_rows), :])
     gather_anc.start()
-    pass_on(4)
-    send_sides(1)
-    gather_dinv.finish()
+    gather_dinv.complete()
     loads[7].wait()
     spread = dot(lower[...], dinv_anc_all[...])
     reach[0] = spread.astype(jnp.bfloat16)
     reach[1] = (spread - reach[0].astype(jnp.float32)).astype(jnp.bfloat16)
     pass_on(2)
-    gather_anc.finish()
+    gather_anc.forward()
+    gather_anc.complete()
     anc_sol[...] = dot(dinv_anc_all[span(row, anc_rows), :], anc_all[...]).astype(jnp.bfloat16)
     store_anc = pltpu.make_async_copy(anc_sol, anc_out, local_sem.at[9])
     store_anc.start()
     loads[5].wait()
     result[...] = rhs_high[...] - dot(reach[0], anc_all[...]) - dot(reach[1], anc_all[...])
-    slot = slot_of(layer)
+    slot = final[layer]
     for p in range(PIECES):
         piece = pl.ds(p * cut, cut)
         summed = partial[slot, piece, :]
@@ -448,7 +473,7 @@
     outs = pl.pallas_call(
         functools.partial(kernel, layers),
         out_shape=shapes,
-        in_specs=[pl.BlockSpec(memory_space=pltpu.SMEM)] + [anywhere] * 8,
+        in_specs=[anywhere] * 9,
         out_specs=(anywhere,) * 3,
         scratch_shapes=[
             pltpu.VMEM(dinv_local.shape[1:], bf16),
@@ -473,10 +498,12 @@
             pltpu.VMEM((3, anc_rows, width), bf16),
             pltpu.VMEM((2, anc_rows, width), bf16),
             pltpu.VMEM(rhs_high.shape, f32),
+            pltpu.SMEM(row_blocks.shape, jnp.int32),
             pltpu.SMEM((held,), jnp.int32),
+            pltpu.SMEM((HBLK,), jnp.int32),
             pltpu.SemaphoreType.DMA((256,)),
             pltpu.SemaphoreType.DMA((256,)),
-            pltpu.SemaphoreType.DMA((11,)),
+            pltpu.SemaphoreType.DMA((12,)),
             pltpu.SemaphoreType.REGULAR((2,)),
         ],
         compiler_params=pltpu.CompilerParams(collective_id=0, has_side_effects=True),

time: 65.9 us -> 62.5 us (0.948)
  Pallas kernels: 64.6 us -> 61.6 us
    pallas_call x1, Pallas kernels: 62.9 us -> 59.9 us  [on_device(): pl.pallas_call(functools.partial(kernel, layers), out_shape=shapes, in_sp...]
where the time goes in v3:
time: 62.5 us; the launch traced here: 62.2 us
  Pallas kernels  61.6 us (99%)
  between operations  0.64 us (1%)
    pallas_call x1, Pallas kernels, on_device(): pl.pallas_call(functools.partial(kernel, layers), out_shape=shapes, in_sp...  59.9 us
    pallas_call x1, Pallas kernels, on_device(): pl.pallas_call(hand_over, out_shape=shapes, in_specs=[anywhere] * 3, out_...  1.65 us

profile of v3, /device:TPU:1, one launch (start us, length us, event | category | flops | bytes accessed | tf_op | source)
XLA Modules:
  0.0 62.2 jit_solution(14961888991439276719)
XLA Ops:
  0.6 59.9 %shard_map.112 = (bf16[1,2,32,256]{3,2,1,0:T(8,128)(2,1)}, bf16[32,256]{1,0:T(8,128)(2,1)}, f32[128,256]{1,0:T(8,128)}) custom-call(s32[1,2,8]{2,1,0:T(2,128)} %blocks_hbm.1, bf16[1,2,32,256]{3,2,1,0:T(8,128)(2,1)} %rhs_hbm.1, bf16[1,2,32,1024]{3,2,1,0:T(8,128)(2,1)} %dinv_hbm.1, bf16[1,2,32,1024]{3,2,1,0:T(8,128)(2,1)} %anc_hbm.1, ...), custom_call_target="tpu_custom_call" | custom-call | tf_op jit(solution)/shard_map/pallas_call | solution.py:473
  60.5 1.6 %shard_map.113 = (bf16[1,2,32,256]{3,2,1,0:T(8,128)(2,1)}, bf16[32,256]{1,0:T(8,128)(2,1)}, f32[128,256]{1,0:T(8,128)}) custom-call(bf16[1,2,32,256]{3,2,1,0:T(8,128)(2,1)} %get-tuple-element.6.refs_0_, bf16[32,256]{1,0:T(8,128)(2,1)} %get-tuple-element.7.refs_1_, f32[128,256]{1,0:T(8,128)} %get-tuple-element.8.refs_2_), custom_call_target="tpu_custom_call" | custom-call | tf_op jit(solution)/shard_map/pallas_call | solution.py:511

commit v4 on v3

--- a/solution.py
+++ b/solution.py
@@ -10,7 +10,7 @@
 BLOCK = 128
 HBLK = 16
 X, Y, CORES = 4, 4, 2
-PIECES = 2
+PIECES = 4
 
 
 class Copies:
@@ -46,10 +46,11 @@
             device_id_type=pl.DeviceIdType.MESH,
         ).wait_recv()
 
-    def drain(self):
-        for copy in self.started:
+    def drain(self, count=None):
+        count = len(self.started) if count is None else count
+        for copy in self.started[:count]:
             copy.wait_send()
-        self.started = []
+        self.started = self.started[count:]
 
 
 class Place:
@@ -204,7 +205,6 @@
     rhs_all,
     sol_all,
     anc_all,
-    anc_sol,
     partial,
     product,
     reach,
@@ -215,7 +215,6 @@
     anc_near,
     anc_far,
     anc_own,
-    result,
     blocks_ref,
     before,
     final,
@@ -243,6 +242,15 @@
 
     def shards_of(ref, s):
         return lambda r: ref.at[s, span(r, rows), :]
+
+    barrier = pltpu.get_barrier_semaphore()
+    lines = [(d, 0) for d in (2, 1, 3)] + [(0, d) for d in (2, 1, 3)]
+    along = [1, -1, 2, -2]
+    for step in along:
+        signal(barrier, {"layer": layer_at(step)})
+    for dx, dy in lines:
+        signal(barrier, {"row": place.at(dx, dy)})
+    signal(barrier, {"row": place.at(0, 0, True)})
 
     loads = []
     for n, (src, dst) in enumerate(
@@ -261,15 +269,6 @@
         load = pltpu.make_async_copy(src, dst, local_sem.at[n])
         load.start()
         loads.append(load)
-
-    barrier = pltpu.get_barrier_semaphore()
-    lines = [(d, 0) for d in (2, 1, 3)] + [(0, d) for d in (2, 1, 3)]
-    along = [1, -1, 2, -2]
-    for step in along:
-        signal(barrier, {"layer": layer_at(step)})
-    for dx, dy in lines:
-        signal(barrier, {"row": place.at(dx, dy)})
-    signal(barrier, {"row": place.at(0, 0, True)})
 
     loads[0].wait()
     pl.semaphore_wait(barrier, len(lines) + 1 + len(along))
@@ -308,10 +307,7 @@
         gather_sol[s].start()
     pl.semaphore_wait(relay.at[0], 2)
     signal(relay.at[1], {"layer": layer_at(-4)})
-    store_sol = pltpu.make_async_copy(
-        sol_all.at[:, span(row, rows), :], sol_out.at[0], local_sem.at[11]
-    )
-    store_sol.start()
+    sol_out[0] = sol_all[:, span(row, rows), :]
 
     near = {step: copies.take() for step in (1, -1, -2)}
     loads[2].wait()
@@ -406,8 +402,10 @@
     pass_on(6)
     send_sides(3)
     gather_dinv.forward()
+    sent = len(copies.started)
     pass_on(4)
     send_sides(1)
+    copies.drain(sent)
     for n, step in enumerate(far):
         copies.arrived(far[step], anc_far.at[n], {"layer": layer_at(-step)})
         own = own + anc_far[n].astype(jnp.float32)
@@ -423,36 +421,25 @@
     pass_on(2)
     gather_anc.forward()
     gather_anc.complete()
-    anc_sol[...] = dot(dinv_anc_all[span(row, anc_rows), :], anc_all[...]).astype(jnp.bfloat16)
-    store_anc = pltpu.make_async_copy(anc_sol, anc_out, local_sem.at[9])
-    store_anc.start()
     loads[5].wait()
-    result[...] = rhs_high[...] - dot(reach[0], anc_all[...]) - dot(reach[1], anc_all[...])
+    high_out[...] = rhs_high[...] - dot(reach[0], anc_all[...]) - dot(reach[1], anc_all[...])
     slot = final[layer]
     for p in range(PIECES):
         piece = pl.ds(p * cut, cut)
         summed = partial[slot, piece, :]
         for w in ways:
             summed = arrived(w, 0, p, summed, p == 0)
-        result[piece, :] = result[piece, :] - summed
-    store_high = pltpu.make_async_copy(result, high_out, local_sem.at[10])
-    store_high.start()
+        high_out[piece, :] = high_out[piece, :] - summed
+    anc_out[...] = dot(dinv_anc_all[span(row, anc_rows), :], anc_all[...]).astype(jnp.bfloat16)
     copies.drain()
-    store_sol.wait()
-    store_anc.wait()
-    store_high.wait()
 
 
 def hand_over(*refs):
-    count = len(refs) // 3
-    given, wanted, held = refs[:count], refs[count : 2 * count], refs[2 * count : -1]
-    sem = refs[-1]
-    loads = [pltpu.make_async_copy(a, b, sem.at[0, n]) for n, (a, b) in enumerate(zip(given, held))]
-    stores = [pltpu.make_async_copy(a, b, sem.at[1, n]) for n, (a, b) in enumerate(zip(held, wanted))]
-    for load in loads:
-        load.start()
-    for load, store in zip(loads, stores):
-        load.wait()
+    count = len(refs) // 2
+    stores = [
+        pltpu.make_async_copy(refs[n], refs[count + n], refs[-1].at[n]) for n in range(count)
+    ]
+    for store in stores:
         store.start()
     for store in stores:
         store.wait()
@@ -474,7 +461,7 @@
         functools.partial(kernel, layers),
         out_shape=shapes,
         in_specs=[anywhere] * 9,
-        out_specs=(anywhere,) * 3,
+        out_specs=(pl.BlockSpec(memory_space=pltpu.VMEM),) * 3,
         scratch_shapes=[
             pltpu.VMEM(dinv_local.shape[1:], bf16),
             pltpu.VMEM(lower_anc.shape[1:], bf16),
@@ -486,7 +473,6 @@
             pltpu.VMEM((supers, order, width), bf16),
             pltpu.VMEM((supers, order, width), bf16),
             pltpu.VMEM((anc_order, width), bf16),
-            pltpu.VMEM((anc_rows, width), bf16),
             pltpu.VMEM((held + 1, BLOCK, width), f32),
             pltpu.VMEM((lower_high.shape[2], width), f32),
             pltpu.VMEM((2, BLOCK, anc_order), bf16),
@@ -497,7 +483,6 @@
             pltpu.VMEM((3, anc_rows, width), bf16),
             pltpu.VMEM((3, anc_rows, width), bf16),
             pltpu.VMEM((2, anc_rows, width), bf16),
-            pltpu.VMEM(rhs_high.shape, f32),
             pltpu.SMEM(row_blocks.shape, jnp.int32),
             pltpu.SMEM((held,), jnp.int32),
             pltpu.SMEM((HBLK,), jnp.int32),
@@ -506,15 +491,15 @@
             pltpu.SemaphoreType.DMA((12,)),
             pltpu.SemaphoreType.REGULAR((2,)),
         ],
-        compiler_params=pltpu.CompilerParams(collective_id=0, has_side_effects=True),
-    )(row_blocks, rhs_local, dinv_local, lower_anc, lower_high, rhs_anc, rhs_high, dinv_anc, lower_anc_high)
+        compiler_params=pltpu.CompilerParams(collective_id=0, has_side_effects=True, vmem_limit_bytes=24 << 20),
+    )(*[pltpu.with_memory_space_constraint(a, pltpu.HBM) for a in (row_blocks, rhs_local, dinv_local, lower_anc, lower_high, rhs_anc, rhs_high, dinv_anc, lower_anc_high)])
     return pl.pallas_call(
         hand_over,
         out_shape=shapes,
-        in_specs=[anywhere] * 3,
+        in_specs=[pl.BlockSpec(memory_space=pltpu.VMEM)] * 3,
         out_specs=(anywhere,) * 3,
-        scratch_shapes=[pltpu.VMEM(a.shape, a.dtype) for a in shapes]
-        + [pltpu.SemaphoreType.DMA((2, 3))],
+        scratch_shapes=[pltpu.SemaphoreType.DMA((3,))],
+        compiler_params=pltpu.CompilerParams(vmem_limit_bytes=4 << 20),
     )(*outs)
 
 

time: 62.5 us -> 60.7 us (0.971)
  Pallas kernels: 61.6 us -> 60 us
    pallas_call x1, Pallas kernels: 1.65 us -> 0.7 us  [on_device(): pl.pallas_call(hand_over, out_shape=shapes, in_specs=[pl.BlockSpec(memory...]
    pallas_call x1, Pallas kernels: 59.9 us -> 59.3 us  [on_device(): pl.pallas_call(functools.partial(kernel, layers), out_shape=shapes, in_sp...]
where the time goes in v4:
time: 60.7 us; the launch traced here: 60.6 us
  Pallas kernels  60 us (99%)
  between operations  0.64 us (1%)
    pallas_call x1, Pallas kernels, on_device(): pl.pallas_call(functools.partial(kernel, layers), out_shape=shapes, in_sp...  59.3 us

profile of v4, /device:TPU:1, one launch (start us, length us, event | category | flops | bytes accessed | tf_op | source)
XLA Modules:
  0.0 60.6 jit_solution(4777516520786454966)
XLA Ops:
  0.6 59.3 %shard_map.112 = (bf16[1,2,32,256]{3,2,1,0:T(8,128)(2,1)S(1)}, bf16[32,256]{1,0:T(8,128)(2,1)S(1)}, f32[128,256]{1,0:T(8,128)S(1)}) custom-call(s32[1,2,8]{2,1,0:T(2,128)} %blocks_hbm.1, bf16[1,2,32,256]{3,2,1,0:T(8,128)(2,1)} %rhs_hbm.1, bf16[1,2,32,1024]{3,2,1,0:T(8,128)(2,1)} %dinv_hbm.1, bf16[1,2,32,1024]{3,2,1,0:T(8,128)(2,1)} %anc_hbm.1, ...), custom_call_target="tpu_custom_call" | custom-call | tf_op jit(solution)/shard_map/pallas_call | solution.py:460
  59.9 0.7 %shard_map.113 = (bf16[1,2,32,256]{3,2,1,0:T(8,128)(2,1)}, bf16[32,256]{1,0:T(8,128)(2,1)}, f32[128,256]{1,0:T(8,128)}) custom-call(bf16[1,2,32,256]{3,2,1,0:T(8,128)(2,1)S(1)} %get-tuple-element.6.refs_0_, bf16[32,256]{1,0:T(8,128)(2,1)S(1)} %get-tuple-element.7.refs_1_, f32[128,256]{1,0:T(8,128)S(1)} %get-tuple-element.8.refs_2_), custom_call_target="tpu_custom_call" | custom-call | tf_op jit(solution)/shard_map/pallas_call | solution.py:496

commit v5 on v4

--- a/solution.py
+++ b/solution.py
@@ -60,8 +60,15 @@
         self.x = row // (Y * CORES)
         self.y = (row // CORES) % Y
         self.core = row % CORES
+        self.known = {}
 
     def at(self, dx, dy, flip=False):
+        key = dx % X, dy % Y, flip
+        if key not in self.known:
+            self.known[key] = self.find(*key)
+        return self.known[key]
+
+    def find(self, dx, dy, flip):
         x = lax.rem(self.x + (dx + X), X)
         y = lax.rem(self.y + (dy + Y), Y)
         core = 1 - self.core if flip else self.core
@@ -175,6 +182,23 @@
             self.copies.arrived(
                 self.other[dx, dy], self.shard(at(-dx, -dy, True)), {"row": at(0, 0, True)}
             )
+
+
+class BulkGather(TreeGather):
+    def __init__(self, copies, place, half, both, all_of):
+        super().__init__(copies, place, half, both)
+        self.all_of = all_of
+        self.bulk = self.other[self.order[-1]]
+
+    def send_other(self, dx, dy):
+        if (dx, dy) == self.order[-1]:
+            mine = self.all_of(self.place.core)
+            self.copies.start(self.bulk, mine, mine, {"row": self.place.at(0, 0, True)})
+
+    def complete(self):
+        self.copies.arrived(
+            self.bulk, self.all_of(1 - self.place.core), {"row": self.place.at(0, 0, True)}
+        )
 
 
 def dot(a, b):
@@ -231,8 +255,13 @@
     held = supers * blocks_ref.shape[2]
     anc_rows = rhs_anc.shape[0]
 
+    others = {}
+
     def layer_at(step):
-        return lax.rem(layer + (step + layers), layers)
+        key = step % layers
+        if key not in others:
+            others[key] = lax.rem(layer + key, layers)
+        return others[key]
 
     def signal(sem, where):
         pl.semaphore_signal(sem, inc=1, device_id=where, device_id_type=pl.DeviceIdType.MESH)
@@ -261,7 +290,7 @@
             (high_hbm.at[0], high),
             (rhs_anc_hbm, rhs_anc),
             (rhs_high_hbm, rhs_high),
-            (dinv_anc_hbm, dinv_anc_all.at[span(row, anc_rows), :]),
+            (dinv_anc_hbm, dinv_anc_all.at[row // CORES, row % CORES]),
             (lower_hbm, lower),
             (blocks_hbm, blocks_ref),
         )
@@ -323,13 +352,14 @@
             for n, step in enumerate(near):
                 copies.start(near[step], anc_own.at[0], anc_near.at[n], {"layer": layer_at(step)})
             loads[6].wait()
-            gather_dinv = TreeGather(
+            gather_dinv = BulkGather(
                 copies,
                 place,
                 lambda h, r: dinv_anc_all.at[
-                    pl.ds(pl.multiple_of(r * anc_rows + h * (anc_rows // 2), anc_rows // 2), anc_rows // 2), :
+                    r // CORES, r % CORES, pl.ds(h * (anc_rows // 2), anc_rows // 2), :
                 ],
-                lambda r: dinv_anc_all.at[span(r, anc_rows), :],
+                lambda r: dinv_anc_all.at[r // CORES, r % CORES],
+                lambda core: dinv_anc_all.at[:, core],
             )
             gather_dinv.start()
         product[...] = dot(high[s], sol_all[s])
@@ -401,10 +431,10 @@
     gather_dinv.turn()
     pass_on(6)
     send_sides(3)
-    gather_dinv.forward()
     sent = len(copies.started)
     pass_on(4)
     send_sides(1)
+    gather_dinv.forward()
     copies.drain(sent)
     for n, step in enumerate(far):
         copies.arrived(far[step], anc_far.at[n], {"layer": layer_at(-step)})
@@ -413,12 +443,12 @@
     anc_all[span(row, anc_rows), :] = (rhs_anc[...] - own).astype(jnp.bfloat16)
     gather_anc = DirectGather(copies, place, lambda r: anc_all.at[span(r, anc_rows), :])
     gather_anc.start()
+    pass_on(2)
     gather_dinv.complete()
     loads[7].wait()
-    spread = dot(lower[...], dinv_anc_all[...])
+    spread = dot(lower[...], dinv_anc_all[...].reshape(lower.shape[1], lower.shape[1]))
     reach[0] = spread.astype(jnp.bfloat16)
     reach[1] = (spread - reach[0].astype(jnp.float32)).astype(jnp.bfloat16)
-    pass_on(2)
     gather_anc.forward()
     gather_anc.complete()
     loads[5].wait()
@@ -430,7 +460,7 @@
         for w in ways:
             summed = arrived(w, 0, p, summed, p == 0)
         high_out[piece, :] = high_out[piece, :] - summed
-    anc_out[...] = dot(dinv_anc_all[span(row, anc_rows), :], anc_all[...]).astype(jnp.bfloat16)
+    anc_out[...] = dot(dinv_anc_all[row // CORES, row % CORES], anc_all[...]).astype(jnp.bfloat16)
     copies.drain()
 
 
@@ -468,7 +498,7 @@
             pltpu.VMEM(lower_high.shape[1:], bf16),
             pltpu.VMEM(rhs_anc.shape, f32),
             pltpu.VMEM(rhs_high.shape, f32),
-            pltpu.VMEM((anc_order, anc_order), bf16),
+            pltpu.VMEM((anc_order // anc_rows // CORES, CORES, anc_rows, anc_order), bf16),
             pltpu.VMEM(lower_anc_high.shape, bf16),
             pltpu.VMEM((supers, order, width), bf16),
             pltpu.VMEM((supers, order, width), bf16),

time: 60.7 us -> 60.6 us (level)
  no operation moved by 1% of the time
where the time goes in v5:
time: 60.6 us; the launch traced here: 60.5 us
  Pallas kernels  59.9 us (99%)
  between operations  0.64 us (1%)
    pallas_call x1, Pallas kernels, on_device(): pl.pallas_call(functools.partial(kernel, layers), out_shape=shapes, in_sp...  59.2 us

profile of v5, /device:TPU:1, one launch (start us, length us, event | category | flops | bytes accessed | tf_op | source)
XLA Modules:
  0.0 60.5 jit_solution(16745958920267063306)
XLA Ops:
  0.6 59.2 %shard_map.112 = (bf16[1,2,32,256]{3,2,1,0:T(8,128)(2,1)S(1)}, bf16[32,256]{1,0:T(8,128)(2,1)S(1)}, f32[128,256]{1,0:T(8,128)S(1)}) custom-call(s32[1,2,8]{2,1,0:T(2,128)} %blocks_hbm.1, bf16[1,2,32,256]{3,2,1,0:T(8,128)(2,1)} %rhs_hbm.1, bf16[1,2,32,1024]{3,2,1,0:T(8,128)(2,1)} %dinv_hbm.1, bf16[1,2,32,1024]{3,2,1,0:T(8,128)(2,1)} %anc_hbm.1, ...), custom_call_target="tpu_custom_call" | custom-call | tf_op jit(solution)/shard_map/pallas_call | solution.py:490
  59.8 0.7 %shard_map.113 = (bf16[1,2,32,256]{3,2,1,0:T(8,128)(2,1)}, bf16[32,256]{1,0:T(8,128)(2,1)}, f32[128,256]{1,0:T(8,128)}) custom-call(bf16[1,2,32,256]{3,2,1,0:T(8,128)(2,1)S(1)} %get-tuple-element.6.refs_0_, bf16[32,256]{1,0:T(8,128)(2,1)S(1)} %get-tuple-element.7.refs_1_, f32[128,256]{1,0:T(8,128)S(1)} %get-tuple-element.8.refs_2_), custom_call_target="tpu_custom_call" | custom-call | tf_op jit(solution)/shard_map/pallas_call | solution.py:526
